TPU v7x, 32 devices: a whole 2x2x4 slice. The times are simulated.
32 devices in a mesh: op: 4 (over y, x), str: 8 (over z, core).
Axes of the slice: x: 2, y: 2, z: 4, core: 2. Of those that a mesh axis runs over, the one named last changes fastest.
Arguments:
- coeffs: float32 [4096, 4096], P('str'), may hold values from -6 to 6
- previous: float32 [4096, 4096], P('str'), may hold values from -6 to 6
- block_values: bfloat16 [4, 32, 6, 128, 128], P('op'), may hold values from -0.21875 to 0.21875
- block_cols: int32 [4, 32, 6], P('op'), may hold values from 0 to 31, as said below
Outputs:
- advanced: float32 [4096, 4096], P('str')
Inputs may be any that keep to these rules, and one draw needn't show every extreme that they name: For every term k and block row r, block_cols[k, r, 0] equals r and the 6 entries of block_cols[k, r] are distinct.
All inputs are finite; a program needn't handle non-finite values.
Results may differ from a plain program's by a relative error of at most 0.0003.
Values sent between devices are 32-bit elements; how exact they have to be, the bound alone decides.
A program may use at most 192 MiB of HBM per device.

v0:
```python
import math
import jax
import jax.numpy as jnp
from jax import lax
from jax.sharding import PartitionSpec as P

STEPS = 2


def per_device(coeffs, previous, block_values, block_cols):
    local_terms = block_values.shape[0]
    step_scale = 2.0 / math.sqrt(local_terms * lax.axis_size("op"))
    factors = block_values.astype(jnp.float32)
    row_count, full_width = coeffs.shape
    block_size = block_values.shape[-1]
    block_count = full_width // block_size
    slot_count = block_cols.shape[2]
    regrouped = lax.all_to_all(
        previous.reshape(row_count, block_count, block_size),
        "str",
        split_axis=1,
        concat_axis=0,
        tiled=True,
    )
    earlier = regrouped.reshape(full_width, row_count).T
    current = coeffs
    for step_index in range(STEPS):
        column_list = block_cols[0].reshape(-1)
        term_factors = factors[0]
        gathered = jnp.take(
            current.reshape(row_count, block_count, block_size), column_list, axis=1
        )
        gathered = gathered.reshape(row_count, block_count, slot_count, block_size)
        beta_side = jnp.einsum(
            "arjc,rjoc->aro", gathered, term_factors, precision=lax.Precision.HIGHEST
        )
        received = lax.all_to_all(beta_side, "str", split_axis=1, concat_axis=0, tiled=True)
        group_count = received.shape[1]
        item_count = received.shape[2]
        grouped = jnp.take(
            received.reshape(block_count, block_size, group_count, item_count), column_list, axis=0
        )
        grouped = grouped.reshape(block_count, slot_count, block_size, group_count, item_count)
        result = jnp.einsum(
            "rjoc,rjcnm->nmro", term_factors, grouped, precision=lax.Precision.HIGHEST
        )
        moved = result.reshape(group_count, item_count, full_width)
        summed = moved.reshape(row_count, full_width)
        updated = step_scale * lax.psum(summed, "op") - earlier
        earlier, current = (current, updated)
    return current


def solution(mesh):
    placed = (P("str", None), P("str", None), P("op", None, None, None, None), P("op", None, None))
    return jax.shard_map(
        per_device, mesh=mesh, in_specs=placed, out_specs=P("str", None), check_vma=False
    )
```

profile of v0, /device:TPU:0, one launch (start us, length us, event | category | flops | bytes accessed | tf_op | source)
XLA Modules:
  0.0 1236.2 jit_solution(6269851794979325475)
XLA Ops:
  25.3 22.2 %gather_fusion = f32[192,512,128]{2,1,0:T(8,128)} fusion(f32[512,32,128]{2,0,1:T(8,128)} %copy.27, s32[1024]{0:T(1024)S(1)} %pad_clamp_fusion), kind=kCustom, calls=%fused_computation.clone | custom fusion | bytes 100664064 | tf_op jit(solution)/shard_map/jit(_take)/gather | solution.py:30
  47.6 34.0 %broadcast_select_fusion.3 = f32[192,512,128]{2,1,0:T(8,128)} fusion(f32[192,512,128]{2,1,0:T(8,128)} %gather_fusion, pred[192]{0:T(512)(128)(4,1)S(1)} %compare_and_fusion), kind=kLoop, calls=%fused_computation.7 | loop fusion | flops 12582912 | bytes 100663488 | tf_op jit(solution)/shard_map/jit(_take)/select_n | solution.py:30
  81.6 30.1 %fusion.8 = f32[512,32,128]{2,0,1:T(8,128)} fusion(f32[512,32,6,128]{3,0,2,1:T(8,128)} %bitcast.92, bf16[1,32,6,128,128]{4,3,2,1,0:T(8,128)(2,1)} %param.10), kind=kOutput, calls=%fused_computation.19 | convolution fusion | flops 19327352832 | bytes 65011712 | tf_op jit(solution)/shard_map/arjc,rjoc->aro/dot_general | solution.py:34
  118.1 9.0 copy.31
  127.1 175.0 %all-to-all-done = f32[512,32,128]{2,0,1:T(8,128)} async-done(((f32[512,32,128]{2,0,1:T(8,128)}), f32[512,32,128]{2,0,1:T(8,128)}, u32[]{:S(2)}, u32[]{:S(2)}) %all-to-all-start) | async-done | bytes 8388640 | tf_op jit(solution)/shard_map/all_to_all | solution.py:37
  314.7 22.2 %gather_fusion.1 = f32[192,128,4,128]{3,1,2,0:T(8,128)} fusion(f32[32,128,4,128]{3,1,0,2:T(8,128)} %bitcast.91, s32[1024]{0:T(1024)S(1)} %pad_clamp_fusion), kind=kCustom, calls=%fused_computation.1.clone | custom fusion | bytes 100664064 | tf_op jit(solution)/shard_map/jit(_take)/gather | solution.py:40
  337.0 34.9 %broadcast_select_fusion.1 = f32[192,128,4,128]{3,1,2,0:T(8,128)} fusion(f32[192,128,4,128]{3,1,2,0:T(8,128)} %gather_fusion.1, pred[192]{0:T(512)(128)(4,1)S(1)} %compare_and_fusion), kind=kLoop, calls=%fused_computation.5 | loop fusion | flops 12582912 | bytes 100663488 | tf_op jit(solution)/shard_map/jit(_take)/select_n | solution.py:40
  371.9 48.2 %fusion.14 = f32[4,128,32,128]{3,1,0,2:T(8,128)} fusion(f32[32,6,128,4,128]{4,2,3,1,0:T(8,128)} %bitcast.95, bf16[1,32,6,128,128]{4,3,2,1,0:T(8,128)(2,1)} %param.10), kind=kOutput, calls=%fused_computation.21 | convolution fusion | flops 19327352832 | bytes 65011712 | tf_op jit(solution)/shard_map/rjoc,rjcnm->nmro/dot_general | solution.py:44
  428.4 11.7 copy.55
  440.1 50.7 %all-to-all-done.1 = f32[512,32,128]{0,2,1:T(8,128)} async-done(((f32[512,32,128]{0,2,1:T(8,128)}), f32[512,32,128]{0,2,1:T(8,128)}, u32[]{:S(2)}, u32[]{:S(2)}) %all-to-all-start.1) | async-done | bytes 8388640 | tf_op jit(solution)/shard_map/all_to_all | solution.py:18
  499.2 11.7 copy.50
  511.0 102.6 %all-reduce.3.cloned.1.call-done = f32[512,4096]{1,0:T(8,128)} async-done(((f32[512,4096]{1,0:T(8,128)}), f32[512,4096]{1,0:T(8,128)}) %all-reduce.3.cloned.1.call-update) | async-done | bytes 8388624 | tf_op jit(solution)/shard_map/psum | solution.py:49
  613.6 11.3 bitcast_subtract_fusion
  624.9 9.0 copy.34
  642.8 22.2 %gather_fusion.2 = f32[192,512,128]{2,1,0:T(8,128)} fusion(f32[512,32,128]{2,0,1:T(8,128)} %copy.35, s32[1024]{0:T(1024)S(1)} %pad_clamp_fusion), kind=kCustom, calls=%fused_computation.2.clone | custom fusion | bytes 100664064 | tf_op jit(solution)/shard_map/jit(_take)/gather | solution.py:30
  665.0 34.0 %broadcast_select_fusion.2 = f32[192,512,128]{2,1,0:T(8,128)} fusion(f32[192,512,128]{2,1,0:T(8,128)} %gather_fusion.2, pred[192]{0:T(512)(128)(4,1)S(1)} %compare_and_fusion), kind=kLoop, calls=%fused_computation.6 | loop fusion | flops 12582912 | bytes 100663488 | tf_op jit(solution)/shard_map/jit(_take)/select_n | solution.py:30
  699.1 30.1 %fusion.11 = f32[512,32,128]{2,0,1:T(8,128)} fusion(f32[512,32,6,128]{3,0,2,1:T(8,128)} %bitcast.93, bf16[1,32,6,128,128]{4,3,2,1,0:T(8,128)(2,1)} %param.10), kind=kOutput, calls=%fused_computation.20 | convolution fusion | flops 19327352832 | bytes 65011712 | tf_op jit(solution)/shard_map/arjc,rjoc->aro/dot_general | solution.py:34
  729.2 188.9 %all_to_all.45 = f32[512,32,128]{2,0,1:T(8,128)S(1)} all-to-all(f32[512,32,128]{2,0,1:T(8,128)} %fusion.11), channel_id=1, replica_groups=mesh['op'=4,'str'=8] {'str'}, dimensions={1} | all-to-all | bytes 16777216 | tf_op jit(solution)/shard_map/all_to_all | solution.py:37
  922.1 22.2 %gather_fusion.3 = f32[192,128,4,128]{3,1,2,0:T(8,128)} fusion(f32[32,128,4,128]{3,1,0,2:T(8,128)} %bitcast.90, s32[1024]{0:T(1024)S(1)} %pad_clamp_fusion), kind=kCustom, calls=%fused_computation.3.clone | custom fusion | bytes 100664064 | tf_op jit(solution)/shard_map/jit(_take)/gather | solution.py:40
  944.3 34.9 %broadcast_select_fusion = f32[192,128,4,128]{3,1,2,0:T(8,128)} fusion(f32[192,128,4,128]{3,1,2,0:T(8,128)} %gather_fusion.3, pred[192]{0:T(512)(128)(4,1)S(1)} %compare_and_fusion), kind=kLoop, calls=%fused_computation.4 | loop fusion | flops 12582912 | bytes 100663488 | tf_op jit(solution)/shard_map/jit(_take)/select_n | solution.py:40
  979.3 47.8 %fusion.17 = f32[4,128,32,128]{3,1,0,2:T(8,128)} fusion(f32[32,6,128,4,128]{4,2,3,1,0:T(8,128)} %bitcast.94, bf16[1,32,6,128,128]{4,3,2,1,0:T(8,128)(2,1)} %param.10), kind=kOutput, calls=%fused_computation.22 | convolution fusion | flops 19327352832 | bytes 65011712 | tf_op jit(solution)/shard_map/rjoc,rjcnm->nmro/dot_general | solution.py:44
  1035.4 11.8 copy.54
  1047.1 170.5 %all-reduce.5.cloned.1.call-done = f32[512,4096]{1,0:T(8,128)} async-done(((f32[512,4096]{1,0:T(8,128)}), f32[512,4096]{1,0:T(8,128)}) %all-reduce.5.cloned.1.call-update) | async-done | bytes 8388624 | tf_op jit(solution)/shard_map/psum | solution.py:49
  1217.6 11.3 sub.7
  (19 shorter events, 75.6 us)
Async XLA Ops:
  111.7 190.3 %all-to-all-start = ((f32[512,32,128]{2,0,1:T(8,128)}), f32[512,32,128]{2,0,1:T(8,128)}, u32[]{:S(2)}, u32[]{:S(2)}) async-start(f32[512,32,128]{2,0,1:T(8,128)} %fusion.8), calls=%async_computation | async-start | bytes 16777216 | tf_op jit(solution)/shard_map/all_to_all | solution.py:37
  302.1 188.8 %all-to-all-start.1 = ((f32[512,32,128]{0,2,1:T(8,128)}), f32[512,32,128]{0,2,1:T(8,128)}, u32[]{:S(2)}, u32[]{:S(2)}) async-start(f32[512,32,128]{0,2,1:T(8,128)} %bitcast.97), calls=%async_computation.1 | async-start | bytes 16777216 | tf_op jit(solution)/shard_map/all_to_all | solution.py:18
  307.0 306.5 %all-reduce.3.cloned.1.call-start = ((), (), s32[]{:S(2)}) async-start(), calls=%async_computation.3 | async-start | bytes 16777216 | tf_op jit(solution)/shard_map/psum | solution.py:49
  440.1 777.5 %all-reduce.5.cloned.1.call-start = ((), (), s32[]{:S(2)}) async-start(), calls=%async_computation.4 | async-start | bytes 16777216 | tf_op jit(solution)/shard_map/psum | solution.py:49
Sparse Core Ops, SparseCore 0:
  440.2 173.3 all-reduce.2
  1047.3 170.2 all-reduce.4
where the time goes:
time: 1250 us; the launch traced here: 1240 us
  waiting for transfers between devices  499 us (40%)
  local copies, waits for them, and re-layouts  206 us (16%)
  blocking collectives  189 us (15%)
  other arithmetic  161 us (13%)
  matrix products  156 us (12%)
  between operations  13.9 us (1%)
    psum x2, waiting for transfers between devices, per_device(): updated = step_scale * lax.psum(summed, 'op') - earlier  273 us
    all_to_all x1, blocking collectives, per_device(): lax.all_to_all(beta_side, 'str', split_axis=1, concat_axis=0, tiled=True)  189 us
    all_to_all x1, waiting for transfers between devices, per_device(): lax.all_to_all(beta_side, 'str', split_axis=1, concat_axis=0, tiled=True)  175 us
    dot_general x2, matrix products, per_device(): jnp.einsum('rjoc,rjcnm->nmro', term_factors, grouped, precision=lax.Preci...  96.1 us
    select_n x3, other arithmetic, per_device(): jnp.take(received.reshape(block_count, block_size, group_count, item_coun...  69.9 us
    select_n x2, other arithmetic, per_device(): jnp.take(current.reshape(row_count, block_count, block_size), column_list...  68.1 us
    dot_general x2, matrix products, per_device(): jnp.einsum('arjc,rjoc->aro', gathered, term_factors, precision=lax.Precis...  60.2 us
    unnamed x6, local copies, waits for them, and re-layouts  53.9 us
  transfers between devices with their start and end apart: 4, of which 4 were waited for; matrix products, arithmetic and copies ran while one was open for 13% of the time, Pallas kernels for 0%

commit v1 on v0

--- a/solution.py
+++ b/solution.py
@@ -46,7 +46,11 @@
         )
         moved = result.reshape(group_count, item_count, full_width)
         summed = moved.reshape(row_count, full_width)
-        updated = step_scale * lax.psum(summed, "op") - earlier
+
+        def raise_panel_on(obj, along_axis):
+            return jnp.sum(lax.all_gather(obj, along_axis), axis=0)
+
+        updated = step_scale * raise_panel_on(summed, "op") - earlier
         earlier, current = (current, updated)
     return current
 

time: 1250 us -> 1520 us (1.22)
  blocking collectives: 189 us -> 567 us
  waiting for transfers between devices: 499 us -> 377 us
  other arithmetic: 161 us -> 192 us
    all_gather x0 -> x2, waiting for transfers between devices: none -> 377 us  [raise_panel_on(): return jnp.sum(lax.all_gather(obj, along_axis), axis=0)]
    psum x2 -> x0, waiting for transfers between devices: 273 us -> none  [per_device(): updated = step_scale * lax.psum(summed, 'op') - earlier]
    all_to_all x2 -> x0, waiting for transfers between devices: 226 us -> none  [the longest x1 175 us: per_device(): lax.all_to_all(beta_side, 'str', split_axis=1, concat_axis=0, tiled=True)]
    all_to_all x1 -> x2, blocking collectives: 189 us -> 379 us  [per_device(): lax.all_to_all(beta_side, 'str', split_axis=1, concat_axis=0, tiled=True)]
    all_to_all x0 -> x1, blocking collectives: none -> 188 us  [per_device(): lax.all_to_all(previous.reshape(row_count, block_count, block_size), 'str...]
    reduce_sum x0 -> x2, other arithmetic: none -> 31.7 us  [raise_panel_on(): return jnp.sum(lax.all_gather(obj, along_axis), axis=0)]
    unnamed x6 -> x4, local copies, waits for them, and re-layouts: 53.9 us -> 31.1 us
    another operation x0 -> x2, local copies, waits for them, and re-layouts: none -> 18.7 us  [raise_panel_on(): return jnp.sum(lax.all_gather(obj, along_axis), axis=0)]
  transfers between devices with their start and end apart: 4 -> 2, of which waited for: 4 -> 2; matrix products, arithmetic and copies ran while one was open for 13% -> 2% of each run, Pallas kernels for 0% -> 0%
where the time goes in v1:
time: 1520 us; the launch traced here: 1510 us
  blocking collectives  567 us (37%)
  waiting for transfers between devices  377 us (25%)
  local copies, waits for them, and re-layouts  201 us (13%)
  other arithmetic  192 us (13%)
  matrix products  156 us (10%)
    all_to_all x2, blocking collectives, per_device(): lax.all_to_all(beta_side, 'str', split_axis=1, concat_axis=0, tiled=True)  379 us
    all_gather x2, waiting for transfers between devices, raise_panel_on(): return jnp.sum(lax.all_gather(obj, along_axis), axis=0)  377 us
    all_to_all x1, blocking collectives, per_device(): lax.all_to_all(previous.reshape(row_count, block_count, block_size), 'str...  188 us
    dot_general x2, matrix products, per_device(): jnp.einsum('rjoc,rjcnm->nmro', term_factors, grouped, precision=lax.Preci...  95.9 us
    select_n x3, other arithmetic, per_device(): jnp.take(received.reshape(block_count, block_size, group_count, item_coun...  69.9 us
    select_n x2, other arithmetic, per_device(): jnp.take(current.reshape(row_count, block_count, block_size), column_list...  68.1 us
    dot_general x2, matrix products, per_device(): jnp.einsum('arjc,rjoc->aro', gathered, term_factors, precision=lax.Precis...  60.4 us
    gather x2, local copies, waits for them, and re-layouts, per_device(): jnp.take(current.reshape(row_count, block_count, block_size), column_list...  44.5 us
  transfers between devices with their start and end apart: 2, of which 2 were waited for; matrix products, arithmetic and copies ran while one was open for 2% of the time, Pallas kernels for 0%

profile of v1, /device:TPU:0, one launch (start us, length us, event | category | flops | bytes accessed | tf_op | source)
XLA Modules:
  0.0 1507.7 jit_solution(930858758463494106)
XLA Ops:
  25.4 22.2 %gather_fusion = f32[192,512,128]{2,1,0:T(8,128)} fusion(f32[512,32,128]{2,0,1:T(8,128)} %copy.41, s32[1024]{0:T(1024)S(1)} %pad_clamp_fusion), kind=kCustom, calls=%fused_computation.clone | custom fusion | bytes 100664064 | tf_op jit(solution)/shard_map/jit(_take)/gather | solution.py:30
  47.6 34.0 %broadcast_select_fusion.3 = f32[192,512,128]{2,1,0:T(8,128)} fusion(f32[192,512,128]{2,1,0:T(8,128)} %gather_fusion, pred[192]{0:T(512)(128)(4,1)S(1)} %compare_and_fusion), kind=kLoop, calls=%fused_computation.7 | loop fusion | flops 12582912 | bytes 100663488 | tf_op jit(solution)/shard_map/jit(_take)/select_n | solution.py:30
  81.6 30.1 %fusion.8 = f32[512,32,128]{2,0,1:T(8,128)} fusion(f32[512,32,6,128]{3,0,2,1:T(8,128)} %bitcast.86, bf16[1,32,6,128,128]{4,3,2,1,0:T(8,128)(2,1)} %param.10), kind=kOutput, calls=%fused_computation.17 | convolution fusion | flops 19327352832 | bytes 65011712 | tf_op jit(solution)/shard_map/arjc,rjoc->aro/dot_general | solution.py:34
  111.8 190.2 %all_to_all.45 = f32[512,32,128]{2,0,1:T(8,128)S(1)} all-to-all(f32[512,32,128]{2,0,1:T(8,128)} %fusion.8), channel_id=1, replica_groups=mesh['op'=4,'str'=8] {'str'}, dimensions={1} | all-to-all | bytes 16777216 | tf_op jit(solution)/shard_map/all_to_all | solution.py:37
  305.9 22.2 %gather_fusion.1 = f32[192,128,4,128]{3,1,2,0:T(8,128)} fusion(f32[32,128,4,128]{3,1,0,2:T(8,128)} %bitcast.85, s32[1024]{0:T(1024)S(1)} %pad_clamp_fusion), kind=kCustom, calls=%fused_computation.1.clone | custom fusion | bytes 100664064 | tf_op jit(solution)/shard_map/jit(_take)/gather | solution.py:40
  328.2 34.9 %broadcast_select_fusion.1 = f32[192,128,4,128]{3,1,2,0:T(8,128)} fusion(f32[192,128,4,128]{3,1,2,0:T(8,128)} %gather_fusion.1, pred[192]{0:T(512)(128)(4,1)S(1)} %compare_and_fusion), kind=kLoop, calls=%fused_computation.5 | loop fusion | flops 12582912 | bytes 100663488 | tf_op jit(solution)/shard_map/jit(_take)/select_n | solution.py:40
  363.1 47.8 %fusion.14 = f32[4,128,32,128]{3,1,0,2:T(8,128)} fusion(f32[32,6,128,4,128]{4,2,3,1,0:T(8,128)} %bitcast.89, bf16[1,32,6,128,128]{4,3,2,1,0:T(8,128)(2,1)} %param.10), kind=kOutput, calls=%fused_computation.19 | convolution fusion | flops 19327352832 | bytes 65011712 | tf_op jit(solution)/shard_map/rjoc,rjcnm->nmro/dot_general | solution.py:44
  410.9 11.5 copy.44
  441.4 187.9 %all_to_all.46 = f32[512,32,128]{0,2,1:T(8,128)S(1)} all-to-all(f32[512,32,128]{0,2,1:T(8,128)} %bitcast.97), channel_id=1, replica_groups=mesh['op'=4,'str'=8] {'str'}, dimensions={1} | all-to-all | bytes 16777216 | tf_op jit(solution)/shard_map/all_to_all | solution.py:18
  634.2 11.7 copy.63
  645.9 82.0 %all-gather.3.cloned.1.call-done = f32[4,512,4096]{2,1,0:T(8,128)} async-done(((f32[1,512,4096]{2,1,0:T(8,128)}), f32[4,512,4096]{2,1,0:T(8,128)}) %all-gather.3.cloned.1.call-update) | async-done | bytes 33554448 | tf_op jit(solution)/shard_map/all_gather | solution.py:51
  727.8 15.9 %reduce_sum.18 = f32[512,4096]{1,0:T(8,128)} reduce(f32[4,512,4096]{2,1,0:T(8,128)} %all-gather.3.cloned.1.call-done, f32[]{:T(128)} %constant.17.clone.1), dimensions={0}, to_apply=%region_0.3 | reduce | flops 6291456 | bytes 41943044 | tf_op jit(solution)/shard_map/reduce_sum | solution.py:51
  743.7 11.3 bitcast_subtract_fusion
  773.0 22.2 %gather_fusion.2 = f32[192,512,128]{2,1,0:T(8,128)} fusion(f32[512,32,128]{2,0,1:T(8,128)} %copy.49, s32[1024]{0:T(1024)S(1)} %pad_clamp_fusion), kind=kCustom, calls=%fused_computation.2.clone | custom fusion | bytes 100664064 | tf_op jit(solution)/shard_map/jit(_take)/gather | solution.py:30
  795.2 34.0 %broadcast_select_fusion.2 = f32[192,512,128]{2,1,0:T(8,128)} fusion(f32[192,512,128]{2,1,0:T(8,128)} %gather_fusion.2, pred[192]{0:T(512)(128)(4,1)S(1)} %compare_and_fusion), kind=kLoop, calls=%fused_computation.6 | loop fusion | flops 12582912 | bytes 100663488 | tf_op jit(solution)/shard_map/jit(_take)/select_n | solution.py:30
  829.2 30.3 %fusion.11 = f32[512,32,128]{2,0,1:T(8,128)} fusion(f32[512,32,6,128]{3,0,2,1:T(8,128)} %bitcast.87, bf16[1,32,6,128,128]{4,3,2,1,0:T(8,128)(2,1)} %param.10), kind=kOutput, calls=%fused_computation.18 | convolution fusion | flops 19327352832 | bytes 65011712 | tf_op jit(solution)/shard_map/arjc,rjoc->aro/dot_general | solution.py:34
  859.5 188.5 %all_to_all.47 = f32[512,32,128]{2,0,1:T(8,128)S(1)} all-to-all(f32[512,32,128]{2,0,1:T(8,128)} %fusion.11), channel_id=1, replica_groups=mesh['op'=4,'str'=8] {'str'}, dimensions={1} | all-to-all | bytes 16777216 | tf_op jit(solution)/shard_map/all_to_all | solution.py:37
  1051.9 22.2 %gather_fusion.3 = f32[192,128,4,128]{3,1,2,0:T(8,128)} fusion(f32[32,128,4,128]{3,1,0,2:T(8,128)} %bitcast.84, s32[1024]{0:T(1024)S(1)} %pad_clamp_fusion), kind=kCustom, calls=%fused_computation.3.clone | custom fusion | bytes 100664064 | tf_op jit(solution)/shard_map/jit(_take)/gather | solution.py:40
  1074.2 34.9 %broadcast_select_fusion = f32[192,128,4,128]{3,1,2,0:T(8,128)} fusion(f32[192,128,4,128]{3,1,2,0:T(8,128)} %gather_fusion.3, pred[192]{0:T(512)(128)(4,1)S(1)} %compare_and_fusion), kind=kLoop, calls=%fused_computation.4 | loop fusion | flops 12582912 | bytes 100663488 | tf_op jit(solution)/shard_map/jit(_take)/select_n | solution.py:40
  1109.1 48.1 %fusion.17 = f32[4,128,32,128]{3,1,0,2:T(8,128)} fusion(f32[32,6,128,4,128]{4,2,3,1,0:T(8,128)} %bitcast.88, bf16[1,32,6,128,128]{4,3,2,1,0:T(8,128)(2,1)} %param.10), kind=kOutput, calls=%fused_computation.20 | convolution fusion | flops 19327352832 | bytes 65011712 | tf_op jit(solution)/shard_map/rjoc,rjcnm->nmro/dot_general | solution.py:44
  1157.2 11.5 copy.52
  1178.0 295.2 %all-gather.5.cloned.1.call-done = f32[4,512,4096]{2,1,0:T(8,128)} async-done(((f32[1,512,4096]{2,1,0:T(8,128)}), f32[4,512,4096]{2,1,0:T(8,128)}) %all-gather.5.cloned.1.call-update) | async-done | bytes 33554448 | tf_op jit(solution)/shard_map/all_gather | solution.py:51
  1473.2 15.9 %reduce_sum.19 = f32[512,4096]{1,0:T(8,128)} reduce(f32[4,512,4096]{2,1,0:T(8,128)} %all-gather.5.cloned.1.call-done, f32[]{:T(128)} %constant.17.clone.1), dimensions={0}, to_apply=%region_1.0 | reduce | flops 6291456 | bytes 41943044 | tf_op jit(solution)/shard_map/reduce_sum | solution.py:51
  1489.1 11.3 sub.7
  (19 shorter events, 78.0 us)
Async XLA Ops:
  6.5 721.3 %all-gather.3.cloned.1.call-start = ((), (), s32[]{:S(2)}) async-start(), calls=%async_computation.3 | async-start | bytes 41943040 | tf_op jit(solution)/shard_map/all_gather | solution.py:51
  431.7 1041.5 %all-gather.5.cloned.1.call-start = ((), (), s32[]{:S(2)}) async-start(), calls=%async_computation.4 | async-start | bytes 41943040 | tf_op jit(solution)/shard_map/all_gather | solution.py:51
Sparse Core Ops, SparseCore 0:
  431.9 295.9 all-gather.2
  1178.1 295.0 all-gather.4
